TPU v7x, 32 devices: a whole 2x2x4 slice. The times are simulated.
32 devices in a mesh: row: 8 (over z, y), col: 4 (over x, core).
Axes of the slice: x: 2, y: 2, z: 4, core: 2. Of those that a mesh axis runs over, the one named last changes fastest.
Arguments:
- queries: bfloat16 [12288, 4096], P(('row', 'col')), may hold values from -6 to 6
- keys: bfloat16 [16384, 256], P(('row', 'col')), may hold values from -6 to 6
- values: bfloat16 [16384, 256], P(('row', 'col')), may hold values from -6 to 6
- output_gradient: bfloat16 [12288, 4096], P(('row', 'col')), may hold values from -6 to 6
- tile_block_table: int32 [96, 3], P(('row', 'col')), may hold values from 0 to 31, as said below
Outputs:
- dqueries: bfloat16 [12288, 4096], P(('row', 'col'))
- dkeys: bfloat16 [16384, 256], P(('row', 'col'))
- dvalues: bfloat16 [16384, 256], P(('row', 'col'))
Inputs may be any that keep to these rules, and one draw needn't show every extreme that they name: `tile_block_table`: A tile's first id is the block that holds its own query rows; its 3 ids are distinct and none is larger than that block. Block b is held by the device of index b // 1 in the order row-major over (row, col). The tiles of one device name at most 1 distinct blocks held on devices of one col index, and at most 2 distinct blocks held on devices of one row index.
All inputs are finite; a program needn't handle non-finite values.
Results may differ from a plain program's by a relative error of at most 0.0064.
Values may be sent and summed in bfloat16 or wider, within the bound.
No kernel may reach another device: no remote copies, remote signals or barrier semaphores. Data moves between devices by JAX's collectives and lax.ppermute only.
A program may use at most 192 MiB of HBM per device.

v0:
```python
import jax
import jax.numpy as jnp
from jax import lax
from jax.sharding import PartitionSpec as P

QUERY_HEADS = 32
KEY_VALUE_HEADS = 2
HEAD_WIDTH = 128
GROUP_WIDTH = 16
TILE_QUERY_ROWS = 128
BLOCK_KEY_ROWS = 512
PICKED_BLOCKS = 3


def pair_grads(
    tile_query_rows, gradient_rows, block_key_rows, block_value_rows, query_place, key_place
):
    factor = HEAD_WIDTH ** (-0.5)
    forward = (((1,), (1,)), ((), ()))
    backward = (((0,), (0,)), ((), ()))
    scores = (
        lax.dot_general(
            tile_query_rows, block_key_rows, forward, preferred_element_type=jnp.float32
        )
        * factor
    )
    scores = jnp.where(key_place[None, :] <= query_place[:, None], scores, -jnp.inf)
    weights = jax.nn.softmax(scores, axis=-1)
    grad_weights = lax.dot_general(
        gradient_rows, block_value_rows, forward, preferred_element_type=jnp.float32
    )
    row_delta = jnp.sum(weights * grad_weights, axis=-1, keepdims=True)
    grad_scores = (weights * (grad_weights - row_delta) * factor).astype(jnp.bfloat16)
    query_gradient = jnp.dot(grad_scores, block_key_rows, preferred_element_type=jnp.float32)
    key_gradient = lax.dot_general(
        grad_scores, tile_query_rows, backward, preferred_element_type=jnp.float32
    )
    value_gradient = lax.dot_general(
        weights.astype(jnp.bfloat16), gradient_rows, backward, preferred_element_type=jnp.float32
    )
    return (query_gradient, key_gradient, value_gradient)


def item_grads(packed):
    query_item, gradient_item, block_item, query_place, key_place = packed
    return pair_grads(
        query_item, gradient_item, block_item[0], block_item[1], query_place, key_place
    )


def local(queries, keys, values, output_gradient, tile_block_table):
    n_row = lax.axis_size("row")
    n_col = lax.axis_size("col")
    my_row = lax.axis_index("row")
    my_col = lax.axis_index("col")
    devices = n_row * n_col
    my_device = my_row * n_col + my_col
    blk_dev = keys.shape[0] // BLOCK_KEY_ROWS
    device_tile_count = tile_block_table.shape[0]
    kv_width = keys.shape[1]
    cap_row = 2 * blk_dev
    nblocks = devices * blk_dev
    band_rows = n_row * blk_dev
    flat_width = BLOCK_KEY_ROWS * 2 * kv_width
    starting_position = nblocks * BLOCK_KEY_ROWS - devices * device_tile_count * TILE_QUERY_ROWS
    catalog = jnp.arange(nblocks, dtype=jnp.int32)
    row_lists = lax.all_gather(tile_block_table, "col", axis=0, tiled=True)
    wanted = jnp.any(
        row_lists.reshape(n_col, device_tile_count * PICKED_BLOCKS, 1) == catalog, axis=1
    ).astype(jnp.int32)
    layout = wanted.reshape(n_col, n_row, n_col, blk_dev)
    by_col = jnp.transpose(layout, (0, 2, 1, 3)).reshape(n_col, n_col, band_rows)
    col_rank = jnp.cumsum(by_col, axis=2) - by_col
    local_kv = jnp.concatenate((keys, values), axis=1)
    column = lax.all_gather(local_kv, "row", axis=0, tiled=True).reshape(band_rows, flat_width)
    row_wants = by_col[:, my_col, :]
    row_ranks = col_rank[:, my_col, :]
    slot_ids = jnp.arange(blk_dev, dtype=jnp.int32)
    picker = (row_ranks[:, None, :] == slot_ids[None, :, None]) & (row_wants[:, None, :] == 1)
    picker = picker.astype(jnp.bfloat16).reshape(n_col * blk_dev, band_rows)
    outgoing = jnp.dot(picker, column, preferred_element_type=jnp.float32).astype(jnp.bfloat16)
    landed_parts = lax.all_to_all(
        outgoing.reshape(n_col, blk_dev, flat_width), "col", split_axis=0, concat_axis=0, tiled=True
    )
    landed_parts = landed_parts.reshape(n_col * blk_dev, BLOCK_KEY_ROWS, 2 * kv_width)
    my_lists = tile_block_table.reshape(device_tile_count * PICKED_BLOCKS)
    holder = my_lists // blk_dev
    holder_row = holder // n_col
    holder_col = holder % n_col
    within = my_lists % blk_dev
    my_ranks = col_rank[my_col]
    paired_position = holder_col * blk_dev + my_ranks[holder_col, holder_row * blk_dev + within]
    paired_key_value = jnp.take(landed_parts, paired_position, axis=0).reshape(
        device_tile_count, PICKED_BLOCKS * BLOCK_KEY_ROWS, 2, KEY_VALUE_HEADS, HEAD_WIDTH
    )
    entry_count = device_tile_count * KEY_VALUE_HEADS
    tile_query_rows = queries.reshape(
        device_tile_count, TILE_QUERY_ROWS, KEY_VALUE_HEADS, GROUP_WIDTH, HEAD_WIDTH
    ).transpose(0, 2, 3, 1, 4)
    tile_query_rows = tile_query_rows.reshape(
        entry_count, GROUP_WIDTH * TILE_QUERY_ROWS, HEAD_WIDTH
    )
    gradient_rows = output_gradient.reshape(
        device_tile_count, TILE_QUERY_ROWS, KEY_VALUE_HEADS, GROUP_WIDTH, HEAD_WIDTH
    ).transpose(0, 2, 3, 1, 4)
    gradient_rows = gradient_rows.reshape(entry_count, GROUP_WIDTH * TILE_QUERY_ROWS, HEAD_WIDTH)
    block_rows = paired_key_value.transpose(0, 3, 2, 1, 4).reshape(
        entry_count, 2, PICKED_BLOCKS * BLOCK_KEY_ROWS, HEAD_WIDTH
    )
    global_tile_index = my_device * device_tile_count + jnp.arange(
        device_tile_count, dtype=jnp.int32
    )
    rows_per_head = jnp.arange(GROUP_WIDTH * TILE_QUERY_ROWS, dtype=jnp.int32) % TILE_QUERY_ROWS
    query_place = jnp.repeat(
        starting_position + global_tile_index[:, None] * TILE_QUERY_ROWS + rows_per_head[None, :],
        KEY_VALUE_HEADS,
        axis=0,
    )
    row_offsets = jnp.arange(BLOCK_KEY_ROWS, dtype=jnp.int32)
    key_place = jnp.repeat(
        (tile_block_table[:, :, None] * BLOCK_KEY_ROWS + row_offsets).reshape(
            device_tile_count, PICKED_BLOCKS * BLOCK_KEY_ROWS
        ),
        KEY_VALUE_HEADS,
        axis=0,
    )
    query_gradient, key_gradient, value_gradient = lax.map(
        item_grads, (tile_query_rows, gradient_rows, block_rows, query_place, key_place)
    )
    dqueries = query_gradient.reshape(
        device_tile_count, KEY_VALUE_HEADS, GROUP_WIDTH, TILE_QUERY_ROWS, HEAD_WIDTH
    ).transpose(0, 3, 1, 2, 4)
    dqueries = dqueries.reshape(
        device_tile_count * TILE_QUERY_ROWS, QUERY_HEADS * HEAD_WIDTH
    ).astype(jnp.bfloat16)
    paired_terms = jnp.stack((key_gradient, value_gradient), axis=0).reshape(
        2, device_tile_count, KEY_VALUE_HEADS, PICKED_BLOCKS, BLOCK_KEY_ROWS, HEAD_WIDTH
    )
    paired_terms = paired_terms.transpose(1, 3, 4, 0, 2, 5).reshape(
        device_tile_count * PICKED_BLOCKS, flat_width
    )
    row_span = n_col * blk_dev
    col_lists = lax.all_gather(tile_block_table, "row", axis=0, tiled=True)
    col_wanted = jnp.any(
        col_lists.reshape(n_row, device_tile_count * PICKED_BLOCKS, 1) == catalog, axis=1
    ).astype(jnp.int32)
    by_row = col_wanted.reshape(n_row, n_row, row_span)
    row_rank = jnp.cumsum(by_row, axis=2) - by_row
    own_ranks = row_rank[my_row]
    row_slot = holder_row * cap_row + own_ranks[holder_row, holder_col * blk_dev + within]
    slot_count = n_row * cap_row
    assign = (row_slot[None, :] == jnp.arange(slot_count, dtype=jnp.int32)[:, None]).astype(
        jnp.float32
    )
    partials = jnp.dot(
        assign, paired_terms, precision=lax.Precision.HIGHEST, preferred_element_type=jnp.float32
    ).astype(jnp.bfloat16)
    returned = lax.all_to_all(
        partials.reshape(n_row, cap_row, flat_width), "row", split_axis=0, concat_axis=0, tiled=True
    )
    returned = returned.reshape(slot_count, flat_width)
    sender_wants = by_row[:, my_row, :]
    sender_ranks = row_rank[:, my_row, :]
    row_slot_ids = jnp.arange(cap_row, dtype=jnp.int32)
    collect = (sender_ranks[:, None, :] == row_slot_ids[None, :, None]) & (
        sender_wants[:, None, :] == 1
    )
    collect = collect.astype(jnp.bfloat16).reshape(slot_count, row_span).T
    result = lax.psum_scatter(
        jnp.dot(collect, returned, preferred_element_type=jnp.float32),
        "col",
        scatter_dimension=0,
        tiled=True,
    )
    result = result.reshape(blk_dev * BLOCK_KEY_ROWS, 2 * kv_width)
    return (
        dqueries,
        result[:, :kv_width].astype(jnp.bfloat16),
        result[:, kv_width:].astype(jnp.bfloat16),
    )


def solution(mesh):
    return jax.shard_map(
        local,
        mesh=mesh,
        in_specs=(
            P(("row", "col"), None),
            P(("row", "col"), None),
            P(("row", "col"), None),
            P(("row", "col"), None),
            P(("row", "col"), None),
        ),
        out_specs=(P(("row", "col"), None), P(("row", "col"), None), P(("row", "col"), None)),
        check_vma=False,
    )
```

profile of v0, /device:TPU:0, one launch (start us, length us, event | category | flops | bytes accessed | tf_op | source)
XLA Modules:
  0.0 771.3 jit_solution(15225292182704396535)
XLA Ops:
  9.9 6.3 all-gather
  19.3 66.9 %all-gather.4.cloned.1.call-done = bf16[4096,512]{1,0:T(8,128)(2,1)} async-done(((bf16[512,512]{1,0:T(8,128)(2,1)}), bf16[4096,512]{1,0:T(8,128)(2,1)}) %all-gather.4.cloned.1.call-update) | async-done | bytes 4194320 | tf_op jit(solution)/shard_map/all_gather | solution.py:75
  86.2 6.0 reshape.352
  92.3 4.7 fusion.27
  119.2 26.1 %all-gather.1 = s32[8,3,3]{2,1,0:T(4,128)S(1)} all-gather(s32[1,3,3]{2,1,0:T(4,128)S(1)} %bitcast.153), channel_id=1, replica_groups=mesh['row'=8,'col'=4] {'row'}, dimensions={0}, use_global_device_ids=true | all-gather | bytes 324 | tf_op jit(solution)/shard_map/all_gather | solution.py:143
  150.6 14.8 %reduce.2 = bf16[4,262144]{1,0:T(4,128)(2,1)} reduce(bf16[4,1,262144]{2,1,0:T(2,128)(2,1)} %reshape.399, bf16[]{:T(256)} %constant.180), dimensions={1}, to_apply=%all_to_all.6.reduce_sub_computation | reduce | bytes 4194306 | tf_op jit(solution)/shard_map/all_to_all | solution.py:82
  171.0 7.8 %gather.20 = bf16[3,1536,2,2,128]{4,3,2,1,0:T(2,128)(2,1)} reshape(bf16[9,512,512]{2,1,0:T(8,128)(2,1)} %gather_fusion.1) | data formatting | bytes 9437184 | tf_op jit(solution)/shard_map/jit(_take)/gather | solution.py:93
  178.8 11.5 %fusion.29 = bf16[3,2,2,1536,128]{4,1,2,3,0:T(2,128)(2,1)S(1)} fusion(bf16[3,1536,2,2,128]{4,3,2,1,0:T(2,128)(2,1)} %gather.20, pred[3,1536]{1,0:T(4,128)(4,1)S(1)} %bitcast.154), kind=kLoop, calls=%fused_computation.42 | loop fusion | flops 2359296 | bytes 9441792 | tf_op jit(solution)/shard_map/transpose | solution.py:107
  193.2 226.3 %while.14 = (s32[]{:T(128)}, bf16[6,2048,128]{2,1,0:T(8,128)(2,1)S(1)}, f32[6,1536,128]{2,1,0:T(8,128)}, f32[6,1536,128]{2,1,0:T(8,128)}, s32[6,1536]{1,0:T(8,12...) while((s32[]{:T(128)}, ...), condition=%wide.region_6.7_spmd, body=%wide.region_2.6_spmd.sunk | while | flops 4086294528 | bytes 213654736 | solution.py:127
  205.8 12.0 %multiply_reduce_fusion.2 = (f32[2048]{0:T(1024)S(1)}, f32[2048,1536]{0,1:T(8,128)}) fusion(f32[2048]{0:T(1024)S(1)} %fusion.73, f32[2048,1536]{0,1:T(8,128)} %copy-done, f32[2048]{0:T(1024)S(1)} %get-tuple-element.142, bf16[6,2,1536,128]{3,2,1,0:T(8,128)(2,1)} %get-tuple-element.176, s32[]{:T(128)} %get-tuple-element.157, s32[]{:T(128)S(6)} %add.285, ...), kind=kOutput, calls=%fused_computation.4.clone.1 | convolution fusion | flops 817887232 | bytes 26108932 | tf_op jit(solution)/shard_map/while/body/eval_jaxpr/dot_general | solution.py:29
  217.8 6.7 multiply_convert_fusion.2
  243.5 12.0 %multiply_reduce_fusion.2 = (f32[2048]{0:T(1024)S(1)}, f32[2048,1536]{0,1:T(8,128)}) fusion(f32[2048]{0:T(1024)S(1)} %fusion.73, f32[2048,1536]{0,1:T(8,128)} %copy-done, f32[2048]{0:T(1024)S(1)} %get-tuple-element.142, bf16[6,2,1536,128]{3,2,1,0:T(8,128)(2,1)} %get-tuple-element.176, s32[]{:T(128)} %get-tuple-element.157, s32[]{:T(128)S(6)} %add.285, ...), kind=kOutput, calls=%fused_computation.4.clone.1 | convolution fusion | flops 817887232 | bytes 26108932 | tf_op jit(solution)/shard_map/while/body/eval_jaxpr/dot_general | solution.py:29
  255.5 6.7 multiply_convert_fusion.2
  281.1 12.0 %multiply_reduce_fusion.2 = (f32[2048]{0:T(1024)S(1)}, f32[2048,1536]{0,1:T(8,128)}) fusion(f32[2048]{0:T(1024)S(1)} %fusion.73, f32[2048,1536]{0,1:T(8,128)} %copy-done, f32[2048]{0:T(1024)S(1)} %get-tuple-element.142, bf16[6,2,1536,128]{3,2,1,0:T(8,128)(2,1)} %get-tuple-element.176, s32[]{:T(128)} %get-tuple-element.157, s32[]{:T(128)S(6)} %add.285, ...), kind=kOutput, calls=%fused_computation.4.clone.1 | convolution fusion | flops 817887232 | bytes 26108932 | tf_op jit(solution)/shard_map/while/body/eval_jaxpr/dot_general | solution.py:29
  293.1 6.7 multiply_convert_fusion.2
  318.7 12.0 %multiply_reduce_fusion.2 = (f32[2048]{0:T(1024)S(1)}, f32[2048,1536]{0,1:T(8,128)}) fusion(f32[2048]{0:T(1024)S(1)} %fusion.73, f32[2048,1536]{0,1:T(8,128)} %copy-done, f32[2048]{0:T(1024)S(1)} %get-tuple-element.142, bf16[6,2,1536,128]{3,2,1,0:T(8,128)(2,1)} %get-tuple-element.176, s32[]{:T(128)} %get-tuple-element.157, s32[]{:T(128)S(6)} %add.285, ...), kind=kOutput, calls=%fused_computation.4.clone.1 | convolution fusion | flops 817887232 | bytes 26108932 | tf_op jit(solution)/shard_map/while/body/eval_jaxpr/dot_general | solution.py:29
  330.7 6.7 multiply_convert_fusion.2
  356.3 12.0 %multiply_reduce_fusion.2 = (f32[2048]{0:T(1024)S(1)}, f32[2048,1536]{0,1:T(8,128)}) fusion(f32[2048]{0:T(1024)S(1)} %fusion.73, f32[2048,1536]{0,1:T(8,128)} %copy-done, f32[2048]{0:T(1024)S(1)} %get-tuple-element.142, bf16[6,2,1536,128]{3,2,1,0:T(8,128)(2,1)} %get-tuple-element.176, s32[]{:T(128)} %get-tuple-element.157, s32[]{:T(128)S(6)} %add.285, ...), kind=kOutput, calls=%fused_computation.4.clone.1 | convolution fusion | flops 817887232 | bytes 26108932 | tf_op jit(solution)/shard_map/while/body/eval_jaxpr/dot_general | solution.py:29
  368.3 6.7 multiply_convert_fusion.2
  393.9 12.0 %multiply_reduce_fusion.2 = (f32[2048]{0:T(1024)S(1)}, f32[2048,1536]{0,1:T(8,128)}) fusion(f32[2048]{0:T(1024)S(1)} %fusion.73, f32[2048,1536]{0,1:T(8,128)} %copy-done, f32[2048]{0:T(1024)S(1)} %get-tuple-element.142, bf16[6,2,1536,128]{3,2,1,0:T(8,128)(2,1)} %get-tuple-element.176, s32[]{:T(128)} %get-tuple-element.157, s32[]{:T(128)S(6)} %add.285, ...), kind=kOutput, calls=%fused_computation.4.clone.1 | convolution fusion | flops 817887232 | bytes 26108932 | tf_op jit(solution)/shard_map/while/body/eval_jaxpr/dot_general | solution.py:29
  405.9 6.7 multiply_convert_fusion.2
  419.6 7.1 copy.68
  426.7 6.0 copy.69
  432.7 5.5 maximum_bitcast_fusion
  438.2 22.1 %reshape.359 = f32[9,262144]{1,0:T(8,128)} reshape(f32[3,3,512,2,2,128]{5,4,3,2,1,0:T(2,128)} %maximum_bitcast_fusion) | data formatting | bytes 18874368 | tf_op jit(solution)/shard_map/reshape | solution.py:139
  460.3 13.9 %convolution_convert_fusion = bf16[16,262144]{1,0:T(8,128)(2,1)} fusion(f32[9,262144]{1,0:T(8,128)} %reshape.359, s32[9]{0:T(128)S(1)} %copy-done.8), kind=kOutput, calls=%fused_computation.35 | convolution fusion | flops 457179264 | bytes 17825828 | tf_op jit(solution)/shard_map/dot_general | solution.py:155
  474.2 9.7 %reshape.360 = bf16[8,2,262144]{2,1,0:T(2,128)(2,1)} reshape(bf16[16,262144]{1,0:T(8,128)(2,1)} %convolution_convert_fusion) | data formatting | bytes 16777216 | tf_op jit(solution)/shard_map/reshape | solution.py:159
  483.9 5.1 all-to-all-start.1
  498.2 170.2 %all-to-all-done.1 = bf16[8,2,262144]{2,1,0:T(2,128)(2,1)} async-done(((bf16[8,2,262144]{2,1,0:T(2,128)(2,1)}), bf16[8,2,262144]{2,1,0:T(2,128)(2,1)}, u32[]{:S(2)}, u32[]{:S(2)}) %all-to-all-start.1) | async-done | bytes 8388640 | tf_op jit(solution)/shard_map/all_to_all | solution.py:158
  668.4 10.5 %convolution_bitcast_fusion.2 = f32[4,262144]{1,0:T(4,128)} fusion(bf16[8,2,262144]{2,1,0:T(2,128)(2,1)} %all-to-all-done.1, s32[8,4]{0,1:T(4,128)S(1)} %dynamic-slice_bitcast_fusion.5, pred[8,4]{0,1:T(4,128)(4,1)S(1)} %fusion.43), kind=kOutput, calls=%fused_computation.36 | convolution fusion | flops 33554560 | bytes 12583072 | tf_op jit(solution)/shard_map/dot_general | solution.py:170
  678.9 76.0 %all-reduce.2 = bf16[4,262144]{1,0:T(4,128)(2,1)S(1)} all-reduce(f32[4,262144]{1,0:T(4,128)} %convolution_bitcast_fusion.2), channel_id=2, replica_groups=mesh['row'=8,'col'=4] {'col'}, use_global_device_ids=true, to_apply=%region_9.10.clone | all-reduce | flops 1048576 | bytes 6291456
  754.9 8.3 %fusion.30 = bf16[262144]{0:T(1024)(128)(2,1)S(1)} fusion(bf16[4,262144]{1,0:T(4,128)(2,1)S(1)} %all-reduce.2, u32[]{:T(128)} %bitcast.35), kind=kLoop, calls=%fused_computation.46 | loop fusion | bytes 1048580 | tf_op jit(solution)/shard_map/convert.3
  (154 shorter events, 165.1 us)
Async XLA Ops:
  7.2 79.1 %all-gather.4.cloned.1.call-start = ((), (), s32[]{:S(2)}) async-start(), calls=%async_computation.2 | async-start | bytes 4718592 | tf_op jit(solution)/shard_map/all_gather | solution.py:75
  102.0 7.4 copy-start.7
  105.5 41.8 %all-to-all-start = ((bf16[4,2,131072]{2,1,0:T(2,128)(2,1)}), bf16[4,2,131072]{2,1,0:T(2,128)(2,1)S(1)}, u32[]{:S(2)}, u32[]{:S(2)}) async-start(bf16[4,2,131072]{2,1,0:T(2,128)(2,1)} %reshape.398), calls=%async_computation | async-start | bytes 4194304 | tf_op jit(solution)/shard_map/all_to_all | solution.py:82
  112.4 2.9 copy-start.2
  145.7 19.8 %copy-start.5 = (s32[8,32]{0,1:T(8,128)}, s32[8,32]{0,1:T(8,128)S(1)}, u32[]{:S(2)}) copy-start(s32[8,32]{0,1:T(8,128)S(1)} %copy.66) | copy-start | bytes 3076
  145.7 19.7 %copy-start.6 = (s32[8,8,4]{0,2,1:T(4,128)}, s32[8,8,4]{0,2,1:T(4,128)S(1)}, u32[]{:S(2)}) copy-start(s32[8,8,4]{0,2,1:T(4,128)S(1)} %sub.31) | copy-start | bytes 3076
  190.3 2.9 copy-start.3
  197.2 4.6 copy-start
  205.8 12.0 %copy-start.1 = (f32[2048,1536]{0,1:T(8,128)S(1)}, f32[2048,1536]{0,1:T(8,128)}, u32[]{:S(2)}) copy-start(f32[2048,1536]{0,1:T(8,128)} %copy-done) | copy-start | bytes 37748740 | tf_op jit(solution)/shard_map/while
  234.9 4.6 copy-start
  243.5 12.0 %copy-start.1 = (f32[2048,1536]{0,1:T(8,128)S(1)}, f32[2048,1536]{0,1:T(8,128)}, u32[]{:S(2)}) copy-start(f32[2048,1536]{0,1:T(8,128)} %copy-done) | copy-start | bytes 37748740 | tf_op jit(solution)/shard_map/while
  272.5 4.6 copy-start
  281.1 12.0 %copy-start.1 = (f32[2048,1536]{0,1:T(8,128)S(1)}, f32[2048,1536]{0,1:T(8,128)}, u32[]{:S(2)}) copy-start(f32[2048,1536]{0,1:T(8,128)} %copy-done) | copy-start | bytes 37748740 | tf_op jit(solution)/shard_map/while
  310.1 4.6 copy-start
  318.7 12.0 %copy-start.1 = (f32[2048,1536]{0,1:T(8,128)S(1)}, f32[2048,1536]{0,1:T(8,128)}, u32[]{:S(2)}) copy-start(f32[2048,1536]{0,1:T(8,128)} %copy-done) | copy-start | bytes 37748740 | tf_op jit(solution)/shard_map/while
  347.7 4.6 copy-start
  356.3 12.0 %copy-start.1 = (f32[2048,1536]{0,1:T(8,128)S(1)}, f32[2048,1536]{0,1:T(8,128)}, u32[]{:S(2)}) copy-start(f32[2048,1536]{0,1:T(8,128)} %copy-done) | copy-start | bytes 37748740 | tf_op jit(solution)/shard_map/while
  385.3 4.6 copy-start
  393.9 12.0 %copy-start.1 = (f32[2048,1536]{0,1:T(8,128)S(1)}, f32[2048,1536]{0,1:T(8,128)}, u32[]{:S(2)}) copy-start(f32[2048,1536]{0,1:T(8,128)} %copy-done) | copy-start | bytes 37748740 | tf_op jit(solution)/shard_map/while
  419.5 7.1 copy-start.4
  438.2 22.1 %copy-start.8 = (s32[9]{0:T(128)S(1)}, s32[9]{0:T(128)}, u32[]{:S(2)}) copy-start(s32[9]{0:T(128)} %multiply_add_fusion) | copy-start | bytes 112
  483.9 5.1 copy-start.9
  483.9 184.5 %all-to-all-start.1 = ((bf16[8,2,262144]{2,1,0:T(2,128)(2,1)}), bf16[8,2,262144]{2,1,0:T(2,128)(2,1)}, u32[]{:S(2)}, u32[]{:S(2)}) async-start(bf16[8,2,262144]{2,1,0:T(2,128)(2,1)} %reshape.360), calls=%async_computation.1 | async-start | bytes 16777216 | tf_op jit(solution)/shard_map/all_to_all | solution.py:158
Sparse Core Ops, SparseCore 0:
  10.7 75.5 all-gather.3
where the time goes:
time: 780 us; the launch traced here: 771 us
  waiting for transfers between devices  237 us (30%)
  matrix products  187 us (24%)
  local copies, waits for them, and re-layouts  122 us (16%)
  blocking collectives  108 us (14%)
  other arithmetic  92.4 us (12%)
  between operations  14.6 us (2%)
  starting transfers between devices  9.03 us (1%)
    all_to_all x1, waiting for transfers between devices, local(): lax.all_to_all(partials.reshape(n_row, cap_row, flat_width), 'row', split...  170 us
    unnamed x1, blocking collectives  76 us
    dot_general x6, matrix products, pair_grads(): lax.dot_general(gradient_rows, block_value_rows, forward, preferred_eleme...  72.1 us
    all_gather x1, waiting for transfers between devices, local(): lax.all_gather(local_kv, 'row', axis=0, tiled=True)  66.9 us
    convert_element_type x6, other arithmetic, pair_grads(): (weights * (grad_weights - row_delta) * factor).astype(jnp.bfloat16)  40 us
    all_gather x1, blocking collectives, local(): col_lists = lax.all_gather(tile_block_table, 'row', axis=0, tiled=True)  26.1 us
    dot_general x6, matrix products, pair_grads(): lax.dot_general(weights.astype(jnp.bfloat16), gradient_rows, backward, pr...  24.1 us
    dot_general x6, matrix products, pair_grads(): lax.dot_general(grad_scores, tile_query_rows, backward, preferred_element...  22.7 us
  transfers between devices with their start and end apart: 3, of which 2 were waited for; matrix products, arithmetic and copies ran while one was open for 3% of the time, Pallas kernels for 0%

commit v1 on v0

--- a/solution.py
+++ b/solution.py
@@ -10,6 +10,18 @@
 TILE_QUERY_ROWS = 128
 BLOCK_KEY_ROWS = 512
 PICKED_BLOCKS = 3
+
+
+def gather_by_bits(x, axis, dim):
+    ways, here, hop = (lax.axis_size(axis), lax.axis_index(axis), x.shape[dim])
+    line, have = (x, 1)
+    while have < ways:
+        line = jnp.concatenate(
+            [line, lax.ppermute(line, axis, [(d, (d - have) % ways) for d in range(ways)])],
+            axis=dim,
+        )
+        have = 2 * have
+    return jnp.roll(line, here * hop, axis=dim)
 
 
 def pair_grads(
@@ -72,7 +84,7 @@
     by_col = jnp.transpose(layout, (0, 2, 1, 3)).reshape(n_col, n_col, band_rows)
     col_rank = jnp.cumsum(by_col, axis=2) - by_col
     local_kv = jnp.concatenate((keys, values), axis=1)
-    column = lax.all_gather(local_kv, "row", axis=0, tiled=True).reshape(band_rows, flat_width)
+    column = gather_by_bits(local_kv, "row", 0).reshape(band_rows, flat_width)
     row_wants = by_col[:, my_col, :]
     row_ranks = col_rank[:, my_col, :]
     slot_ids = jnp.arange(blk_dev, dtype=jnp.int32)

time: 780 us -> 838 us (1.074)
  waiting for transfers between devices: 237 us -> 285 us
  local copies, waits for them, and re-layouts: 122 us -> 138 us
  between operations: 14.6 us -> 1.21 us
    ppermute x0 -> x3, waiting for transfers between devices: none -> 114 us  [gather_by_bits(): lax.ppermute(line, axis, [(d, (d - have) % ways) for d in range(ways)])]
    all_gather x1 -> x0, waiting for transfers between devices: 66.9 us -> none  [local(): lax.all_gather(local_kv, 'row', axis=0, tiled=True)]
    unnamed x26 -> x42, local copies, waits for them, and re-layouts: 13.2 us -> 22.9 us
  transfers between devices with their start and end apart: 3 -> 5, of which waited for: 2 -> 4; matrix products, arithmetic and copies ran while one was open for 3% -> 3% of each run, Pallas kernels for 0% -> 0%
where the time goes in v1:
time: 838 us; the launch traced here: 828 us
  waiting for transfers between devices  285 us (34%)
  matrix products  187 us (22%)
  local copies, waits for them, and re-layouts  138 us (16%)
  blocking collectives  108 us (13%)
  other arithmetic  91.4 us (11%)
  starting transfers between devices  17.3 us (2%)
    all_to_all x1, waiting for transfers between devices, local(): lax.all_to_all(partials.reshape(n_row, cap_row, flat_width), 'row', split...  170 us
    ppermute x3, waiting for transfers between devices, gather_by_bits(): lax.ppermute(line, axis, [(d, (d - have) % ways) for d in range(ways)])  114 us
    unnamed x1, blocking collectives  76 us
    dot_general x6, matrix products, pair_grads(): lax.dot_general(gradient_rows, block_value_rows, forward, preferred_eleme...  72.1 us
    convert_element_type x6, other arithmetic, pair_grads(): (weights * (grad_weights - row_delta) * factor).astype(jnp.bfloat16)  40 us
    all_gather x1, blocking collectives, local(): col_lists = lax.all_gather(tile_block_table, 'row', axis=0, tiled=True)  26.6 us
    dot_general x6, matrix products, pair_grads(): lax.dot_general(weights.astype(jnp.bfloat16), gradient_rows, backward, pr...  24.1 us
    unnamed x42, local copies, waits for them, and re-layouts  22.9 us
  transfers between devices with their start and end apart: 5, of which 4 were waited for; matrix products, arithmetic and copies ran while one was open for 3% of the time, Pallas kernels for 0%

profile of v1, /device:TPU:0, one launch (start us, length us, event | category | flops | bytes accessed | tf_op | source)
XLA Modules:
  0.0 828.4 jit_solution(13159179320332587707)
XLA Ops:
  4.1 6.0 collective-permute-start
  10.1 11.2 %collective-permute-done = bf16[512,512]{1,0:T(8,128)(2,1)S(1)} collective-permute-done((bf16[512,512]{1,0:T(8,128)(2,1)S(1)}, bf16[512,512]{1,0:T(8,128)(2,1)S(1)}, u32[]{:S(2)}, u32[]{:S(2)}) %collective-permute-start) | collective-permute-done | bytes 524320 | tf_op jit(solution)/shard_map/ppermute | solution.py:20
  29.4 16.0 %collective-permute-done.1 = bf16[1024,512]{1,0:T(8,128)(2,1)S(1)} collective-permute-done((bf16[1024,512]{1,0:T(8,128)(2,1)S(1)}, bf16[1024,512]{1,0:T(8,128)(2,1)S(1)}, u32[]{:S(2)}, u32[]{:S(2)}) %collective-permute-start.1) | collective-permute-done | bytes 1048608 | tf_op jit(solution)/shard_map/ppermute | solution.py:20
  51.8 86.8 %collective-permute-done.2 = bf16[2048,512]{1,0:T(8,128)(2,1)S(1)} collective-permute-done((bf16[2048,512]{1,0:T(8,128)(2,1)}, bf16[2048,512]{1,0:T(8,128)(2,1)S(1)}, u32[]{:S(2)}, u32[]{:S(2)}) %collective-permute-start.2) | collective-permute-done | bytes 2097184 | tf_op jit(solution)/shard_map/ppermute | solution.py:20
  149.4 6.0 reshape.352
  182.6 26.6 %all-gather.1 = s32[8,3,3]{2,1,0:T(4,128)S(1)} all-gather(s32[1,3,3]{2,1,0:T(4,128)S(1)} %bitcast.153), channel_id=1, replica_groups=mesh['row'=8,'col'=4] {'row'}, dimensions={0}, use_global_device_ids=true | all-gather | bytes 324 | tf_op jit(solution)/shard_map/all_gather | solution.py:155
  214.5 14.8 %reduce.2 = bf16[4,262144]{1,0:T(4,128)(2,1)} reduce(bf16[4,1,262144]{2,1,0:T(2,128)(2,1)} %reshape.399, bf16[]{:T(256)} %constant.201), dimensions={1}, to_apply=%all_to_all.6.reduce_sub_computation | reduce | bytes 4194306 | tf_op jit(solution)/shard_map/all_to_all | solution.py:94
  234.9 7.8 gather.20
  242.7 11.5 %fusion.29 = bf16[3,2,2,1536,128]{4,1,2,3,0:T(2,128)(2,1)S(1)} fusion(bf16[3,1536,2,2,128]{4,3,2,1,0:T(2,128)(2,1)} %gather.20, pred[3,1536]{1,0:T(4,128)(4,1)S(1)} %bitcast.154), kind=kLoop, calls=%fused_computation.42 | loop fusion | flops 2359296 | bytes 9441792 | tf_op jit(solution)/shard_map/transpose | solution.py:119
  257.1 226.0 %while.14 = (s32[]{:T(128)}, bf16[6,2048,128]{2,1,0:T(8,128)(2,1)S(1)}, f32[6,1536,128]{2,1,0:T(8,128)}, f32[6,1536,128]{2,1,0:T(8,128)}, s32[6,1536]{1,0:T(8,12...) while((s32[]{:T(128)}, ...), condition=%wide.region_6.7_spmd, body=%wide.region_2.6_spmd.sunk | while | flops 4086294528 | bytes 213654736 | solution.py:139
  269.3 12.0 %multiply_reduce_fusion.2 = (f32[2048]{0:T(1024)S(1)}, f32[2048,1536]{0,1:T(8,128)}) fusion(f32[2048]{0:T(1024)S(1)} %fusion.73, f32[2048,1536]{0,1:T(8,128)} %copy-done, f32[2048]{0:T(1024)S(1)} %get-tuple-element.146, bf16[6,2,1536,128]{3,2,1,0:T(8,128)(2,1)} %get-tuple-element.180, s32[]{:T(128)} %get-tuple-element.161, s32[]{:T(128)S(6)} %add.297, ...), kind=kOutput, calls=%fused_computation.4.clone.1 | convolution fusion | flops 817887232 | bytes 26108932 | tf_op jit(solution)/shard_map/while/body/eval_jaxpr/dot_general | solution.py:41
  281.4 6.7 multiply_convert_fusion.2
  307.0 12.0 %multiply_reduce_fusion.2 = (f32[2048]{0:T(1024)S(1)}, f32[2048,1536]{0,1:T(8,128)}) fusion(f32[2048]{0:T(1024)S(1)} %fusion.73, f32[2048,1536]{0,1:T(8,128)} %copy-done, f32[2048]{0:T(1024)S(1)} %get-tuple-element.146, bf16[6,2,1536,128]{3,2,1,0:T(8,128)(2,1)} %get-tuple-element.180, s32[]{:T(128)} %get-tuple-element.161, s32[]{:T(128)S(6)} %add.297, ...), kind=kOutput, calls=%fused_computation.4.clone.1 | convolution fusion | flops 817887232 | bytes 26108932 | tf_op jit(solution)/shard_map/while/body/eval_jaxpr/dot_general | solution.py:41
  319.0 6.7 multiply_convert_fusion.2
  344.6 12.0 %multiply_reduce_fusion.2 = (f32[2048]{0:T(1024)S(1)}, f32[2048,1536]{0,1:T(8,128)}) fusion(f32[2048]{0:T(1024)S(1)} %fusion.73, f32[2048,1536]{0,1:T(8,128)} %copy-done, f32[2048]{0:T(1024)S(1)} %get-tuple-element.146, bf16[6,2,1536,128]{3,2,1,0:T(8,128)(2,1)} %get-tuple-element.180, s32[]{:T(128)} %get-tuple-element.161, s32[]{:T(128)S(6)} %add.297, ...), kind=kOutput, calls=%fused_computation.4.clone.1 | convolution fusion | flops 817887232 | bytes 26108932 | tf_op jit(solution)/shard_map/while/body/eval_jaxpr/dot_general | solution.py:41
  356.6 6.7 multiply_convert_fusion.2
  382.2 12.0 %multiply_reduce_fusion.2 = (f32[2048]{0:T(1024)S(1)}, f32[2048,1536]{0,1:T(8,128)}) fusion(f32[2048]{0:T(1024)S(1)} %fusion.73, f32[2048,1536]{0,1:T(8,128)} %copy-done, f32[2048]{0:T(1024)S(1)} %get-tuple-element.146, bf16[6,2,1536,128]{3,2,1,0:T(8,128)(2,1)} %get-tuple-element.180, s32[]{:T(128)} %get-tuple-element.161, s32[]{:T(128)S(6)} %add.297, ...), kind=kOutput, calls=%fused_computation.4.clone.1 | convolution fusion | flops 817887232 | bytes 26108932 | tf_op jit(solution)/shard_map/while/body/eval_jaxpr/dot_general | solution.py:41
  394.2 6.7 multiply_convert_fusion.2
  419.8 12.0 %multiply_reduce_fusion.2 = (f32[2048]{0:T(1024)S(1)}, f32[2048,1536]{0,1:T(8,128)}) fusion(f32[2048]{0:T(1024)S(1)} %fusion.73, f32[2048,1536]{0,1:T(8,128)} %copy-done, f32[2048]{0:T(1024)S(1)} %get-tuple-element.146, bf16[6,2,1536,128]{3,2,1,0:T(8,128)(2,1)} %get-tuple-element.180, s32[]{:T(128)} %get-tuple-element.161, s32[]{:T(128)S(6)} %add.297, ...), kind=kOutput, calls=%fused_computation.4.clone.1 | convolution fusion | flops 817887232 | bytes 26108932 | tf_op jit(solution)/shard_map/while/body/eval_jaxpr/dot_general | solution.py:41
  431.8 6.7 multiply_convert_fusion.2
  457.4 12.0 %multiply_reduce_fusion.2 = (f32[2048]{0:T(1024)S(1)}, f32[2048,1536]{0,1:T(8,128)}) fusion(f32[2048]{0:T(1024)S(1)} %fusion.73, f32[2048,1536]{0,1:T(8,128)} %copy-done, f32[2048]{0:T(1024)S(1)} %get-tuple-element.146, bf16[6,2,1536,128]{3,2,1,0:T(8,128)(2,1)} %get-tuple-element.180, s32[]{:T(128)} %get-tuple-element.161, s32[]{:T(128)S(6)} %add.297, ...), kind=kOutput, calls=%fused_computation.4.clone.1 | convolution fusion | flops 817887232 | bytes 26108932 | tf_op jit(solution)/shard_map/while/body/eval_jaxpr/dot_general | solution.py:41
  469.4 6.7 multiply_convert_fusion.2
  483.1 7.1 copy.68
  490.2 6.0 copy.69
  496.2 5.5 maximum_bitcast_fusion
  501.7 22.3 %reshape.359 = f32[9,262144]{1,0:T(8,128)} reshape(f32[3,3,512,2,2,128]{5,4,3,2,1,0:T(2,128)} %maximum_bitcast_fusion) | data formatting | bytes 18874368 | tf_op jit(solution)/shard_map/reshape | solution.py:151
  524.1 13.9 %convolution_convert_fusion = bf16[16,262144]{1,0:T(8,128)(2,1)} fusion(f32[9,262144]{1,0:T(8,128)} %reshape.359, s32[9]{0:T(128)S(1)} %copy-done.12), kind=kOutput, calls=%fused_computation.35 | convolution fusion | flops 457179264 | bytes 17825828 | tf_op jit(solution)/shard_map/dot_general | solution.py:167
  538.0 9.5 %reshape.360 = bf16[8,2,262144]{2,1,0:T(2,128)(2,1)} reshape(bf16[16,262144]{1,0:T(8,128)(2,1)} %convolution_convert_fusion) | data formatting | bytes 16777216 | tf_op jit(solution)/shard_map/reshape | solution.py:171
  561.7 170.5 %all-to-all-done.1 = bf16[8,2,262144]{2,1,0:T(2,128)(2,1)} async-done(((bf16[8,2,262144]{2,1,0:T(2,128)(2,1)}), bf16[8,2,262144]{2,1,0:T(2,128)(2,1)}, u32[]{:S(2)}, u32[]{:S(2)}) %all-to-all-start.1) | async-done | bytes 8388640 | tf_op jit(solution)/shard_map/all_to_all | solution.py:170
  732.2 10.5 %convolution_bitcast_fusion.2 = f32[4,262144]{1,0:T(4,128)} fusion(bf16[8,2,262144]{2,1,0:T(2,128)(2,1)} %all-to-all-done.1, s32[8,4]{0,1:T(4,128)S(1)} %dynamic-slice_bitcast_fusion.5, pred[8,4]{0,1:T(4,128)(4,1)S(1)} %fusion.43), kind=kOutput, calls=%fused_computation.36 | convolution fusion | flops 33554560 | bytes 12583072 | tf_op jit(solution)/shard_map/dot_general | solution.py:182
  742.7 76.0 %all-reduce.2 = bf16[4,262144]{1,0:T(4,128)(2,1)S(1)} all-reduce(f32[4,262144]{1,0:T(4,128)} %convolution_bitcast_fusion.2), channel_id=2, replica_groups=mesh['row'=8,'col'=4] {'col'}, use_global_device_ids=true, to_apply=%region_9.10.clone | all-reduce | flops 1048576 | bytes 6291456
  818.7 8.3 fusion.30
  (177 shorter events, 198.1 us)
Async XLA Ops:
  0.6 46.8 %copy-start.11 = (s32[3,3]{1,0:T(4,128)S(1)}, s32[3,3]{1,0:T(4,128)}, u32[]{:S(2)}) copy-start(s32[3,3]{1,0:T(4,128)} %param.11) | copy-start | bytes 112
  4.1 17.2 %collective-permute-start = (bf16[512,512]{1,0:T(8,128)(2,1)S(1)}, bf16[512,512]{1,0:T(8,128)(2,1)S(1)}, u32[]{:S(2)}, u32[]{:S(2)}) collective-permute-start(bf16[512,512]{1,0:T(8,128)(2,1)S(1)} %get-tuple-element.82), channel_id=1, source_target_pairs={{0,28},{4,0},{8,4},{12,8},{16,12},{20,16},{24,20},{28,24},{1,29},{... | collective-permute-start | bytes 1572872 | tf_op jit(solution)/shard_map/ppermute | solution.py:20
  21.3 24.2 %copy-start.2 = (bf16[512,512]{1,0:T(8,128)(2,1)}, bf16[512,512]{1,0:T(8,128)(2,1)S(1)}, u32[]{:S(2)}) copy-start(bf16[512,512]{1,0:T(8,128)(2,1)S(1)} %collective-permute-done) | copy-start | bytes 1572868
  21.4 118.7 %copy-start.7 = (bf16[512,256]{1,0:T(8,128)(2,1)S(1)}, bf16[512,256]{1,0:T(8,128)(2,1)}, u32[]{:S(2)}) copy-start(bf16[512,256]{1,0:T(8,128)(2,1)} %param.8) | copy-start | bytes 786436
  21.4 24.1 %collective-permute-start.1 = (bf16[1024,512]{1,0:T(8,128)(2,1)S(1)}, bf16[1024,512]{1,0:T(8,128)(2,1)S(1)}, u32[]{:S(2)}, u32[]{:S(2)}) collective-permute-start(bf16[1024,512]{1,0:T(8,128)(2,1)S(1)} %pad_maximum_fusion.1), channel_id=1, source_target_pairs={{0,24},{4,28},{8,0},{12,4},{16,8},{20,12},{24,16},{28,20},{1,25},{... | collective-permute-start | bytes 3145736 | tf_op jit(solution)/shard_map/ppermute | solution.py:20
  46.9 91.7 %collective-permute-start.2 = (bf16[2048,512]{1,0:T(8,128)(2,1)}, bf16[2048,512]{1,0:T(8,128)(2,1)S(1)}, u32[]{:S(2)}, u32[]{:S(2)}) collective-permute-start(bf16[2048,512]{1,0:T(8,128)(2,1)} %pad_maximum_fusion), channel_id=1, source_target_pairs={{0,16},{4,20},{8,24},{12,28},{16,0},{20,4},{24,8},{28,12},{1,17},{... | collective-permute-start | bytes 6291464 | tf_op jit(solution)/shard_map/ppermute | solution.py:20
  48.4 92.4 %copy-start.8 = (bf16[512,256]{1,0:T(8,128)(2,1)S(1)}, bf16[512,256]{1,0:T(8,128)(2,1)}, u32[]{:S(2)}) copy-start(bf16[512,256]{1,0:T(8,128)(2,1)} %param.9) | copy-start | bytes 786436
  48.4 93.2 %copy-start.3 = (bf16[512,512]{1,0:T(8,128)(2,1)S(1)}, bf16[512,512]{1,0:T(8,128)(2,1)}, u32[]{:S(2)}) copy-start(bf16[512,512]{1,0:T(8,128)(2,1)} %copy-done.2) | copy-start | bytes 1572868
  168.6 42.5 %all-to-all-start = ((bf16[4,2,131072]{2,1,0:T(2,128)(2,1)}), bf16[4,2,131072]{2,1,0:T(2,128)(2,1)S(1)}, u32[]{:S(2)}, u32[]{:S(2)}) async-start(bf16[4,2,131072]{2,1,0:T(2,128)(2,1)} %reshape.398), calls=%async_computation | async-start | bytes 4194304 | tf_op jit(solution)/shard_map/all_to_all | solution.py:94
  172.9 5.8 copy-start.4
  209.5 19.8 %copy-start.9 = (s32[8,32]{0,1:T(8,128)}, s32[8,32]{0,1:T(8,128)S(1)}, u32[]{:S(2)}) copy-start(s32[8,32]{0,1:T(8,128)S(1)} %copy.66) | copy-start | bytes 3076
  209.6 19.7 %copy-start.10 = (s32[8,8,4]{0,2,1:T(4,128)}, s32[8,8,4]{0,2,1:T(4,128)S(1)}, u32[]{:S(2)}) copy-start(s32[8,8,4]{0,2,1:T(4,128)S(1)} %sub.36) | copy-start | bytes 3076
  254.2 2.9 copy-start.5
  260.8 4.6 copy-start
  269.3 12.0 %copy-start.1 = (f32[2048,1536]{0,1:T(8,128)S(1)}, f32[2048,1536]{0,1:T(8,128)}, u32[]{:S(2)}) copy-start(f32[2048,1536]{0,1:T(8,128)} %copy-done) | copy-start | bytes 37748740 | tf_op jit(solution)/shard_map/while
  298.4 4.6 copy-start
  307.0 12.0 %copy-start.1 = (f32[2048,1536]{0,1:T(8,128)S(1)}, f32[2048,1536]{0,1:T(8,128)}, u32[]{:S(2)}) copy-start(f32[2048,1536]{0,1:T(8,128)} %copy-done) | copy-start | bytes 37748740 | tf_op jit(solution)/shard_map/while
  336.0 4.6 copy-start
  344.6 12.0 %copy-start.1 = (f32[2048,1536]{0,1:T(8,128)S(1)}, f32[2048,1536]{0,1:T(8,128)}, u32[]{:S(2)}) copy-start(f32[2048,1536]{0,1:T(8,128)} %copy-done) | copy-start | bytes 37748740 | tf_op jit(solution)/shard_map/while
  373.6 4.6 copy-start
  382.2 12.0 %copy-start.1 = (f32[2048,1536]{0,1:T(8,128)S(1)}, f32[2048,1536]{0,1:T(8,128)}, u32[]{:S(2)}) copy-start(f32[2048,1536]{0,1:T(8,128)} %copy-done) | copy-start | bytes 37748740 | tf_op jit(solution)/shard_map/while
  411.2 4.6 copy-start
  419.8 12.0 %copy-start.1 = (f32[2048,1536]{0,1:T(8,128)S(1)}, f32[2048,1536]{0,1:T(8,128)}, u32[]{:S(2)}) copy-start(f32[2048,1536]{0,1:T(8,128)} %copy-done) | copy-start | bytes 37748740 | tf_op jit(solution)/shard_map/while
  448.8 4.6 copy-start
  457.4 12.0 %copy-start.1 = (f32[2048,1536]{0,1:T(8,128)S(1)}, f32[2048,1536]{0,1:T(8,128)}, u32[]{:S(2)}) copy-start(f32[2048,1536]{0,1:T(8,128)} %copy-done) | copy-start | bytes 37748740 | tf_op jit(solution)/shard_map/while
  483.1 13.1 %copy-start.6 = (bf16[6,2048,128]{2,1,0:T(8,128)(2,1)}, bf16[6,2048,128]{2,1,0:T(8,128)(2,1)S(1)}, u32[]{:S(2)}) copy-start(bf16[6,2048,128]{2,1,0:T(8,128)(2,1)S(1)} %get-tuple-element.52) | copy-start | bytes 9437188
  501.7 22.3 %copy-start.12 = (s32[9]{0:T(128)S(1)}, s32[9]{0:T(128)}, u32[]{:S(2)}) copy-start(s32[9]{0:T(128)} %multiply_add_fusion) | copy-start | bytes 112
  547.4 5.1 copy-start.13
  547.4 184.8 %all-to-all-start.1 = ((bf16[8,2,262144]{2,1,0:T(2,128)(2,1)}), bf16[8,2,262144]{2,1,0:T(2,128)(2,1)}, u32[]{:S(2)}, u32[]{:S(2)}) async-start(bf16[8,2,262144]{2,1,0:T(2,128)(2,1)} %reshape.360), calls=%async_computation.1 | async-start | bytes 16777216 | tf_op jit(solution)/shard_map/all_to_all | solution.py:170
